TPU v7x, 32 devices: a whole 2x2x4 slice. The times are simulated.
32 devices in a mesh: rows: 8 (over z, y), cols: 4 (over x, core).
Axes of the slice: x: 2, y: 2, z: 4, core: 2. Of those that a mesh axis runs over, the one named last changes fastest.
Arguments:
- basis_cols: bfloat16 [32768, 1024], P('rows', 'cols'), may hold values from -6 to 6, as said below
- snapshots: bfloat16 [256, 32768], P(None, 'rows'), may hold values from -600 to 600
Outputs:
- coefficients: float32 [1024, 256], P('cols')
- factor: float32 [256, 256], replicated
- directions: bfloat16 [256, 32768], P(None, ('rows', 'cols'))
Inputs may be any that keep to these rules, and one draw needn't show every extreme that they name: `basis_cols`: normal entries.
All inputs are finite; a program needn't handle non-finite values.
Results may differ from a plain program's by a relative error of at most 0.0056.
Values may be sent and summed in bfloat16 or wider, within the bound.
No kernel may reach another device: no remote copies, remote signals or barrier semaphores. Data moves between devices by JAX's collectives and lax.ppermute only.
A program may use at most 64 MiB of HBM per device.

v0:
```python
import math
import jax
import jax.numpy as jnp
from jax import lax
from jax.sharding import PartitionSpec as P

RANK = 1024


def shards(basis_cols, snapshots):
    col_count = lax.axis_size("cols")
    column_index = lax.axis_index("cols")
    total_points = snapshots.shape[1] * lax.axis_size("rows")
    part_rows = snapshots.shape[1] // col_count
    own_snaps = lax.dynamic_slice_in_dim(snapshots, column_index * part_rows, part_rows, 1)
    coeff_scale = math.sqrt(RANK) / total_points
    partial_value = lax.dot_general(
        basis_cols, snapshots, (((0,), (1,)), ((), ())), preferred_element_type=jnp.float32
    )
    coefficients = lax.psum(partial_value, "rows") * coeff_scale
    coeff_low = coefficients.astype(jnp.bfloat16)
    recon_part = lax.dot_general(
        coeff_low, basis_cols, (((0,), (1,)), ((), ())), preferred_element_type=jnp.float32
    )
    recon = lax.psum_scatter(recon_part, "cols", scatter_dimension=1, tiled=True) / math.sqrt(RANK)
    residual = own_snaps.astype(jnp.float32) - recon
    partial_gram = jnp.dot(residual, residual.T, precision=lax.Precision.HIGHEST) / total_points
    gram = lax.psum(partial_gram, ("rows", "cols"))
    factor = jnp.linalg.cholesky(gram)
    directions = lax.linalg.triangular_solve(factor, residual, left_side=True, lower=True).astype(
        jnp.bfloat16
    )
    return (coefficients, factor, directions)


def solution(mesh):
    placed = (P("rows", "cols"), P(None, "rows"))
    return jax.shard_map(
        shards,
        mesh=mesh,
        in_specs=placed,
        out_specs=(P("cols", None), P(), P(None, ("rows", "cols"))),
        check_vma=False,
    )
```

profile of v0, /device:TPU:0, one launch (start us, length us, event | category | flops | bytes accessed | tf_op | source)
XLA Modules:
  0.0 342.6 jit_solution(12605223507592802516)
XLA Ops:
  7.2 1.5 copy-done
  8.8 3.0 fusion.12
  11.9 73.8 %all-reduce.4.cloned.1.call-done = f32[256,256]{1,0:T(8,128)} async-done(((f32[256,256]{1,0:T(8,128)}), f32[256,256]{1,0:T(8,128)}) %all-reduce.4.cloned.1.call-update) | async-done | bytes 262160 | tf_op jit(solution)/shard_map/psum | solution.py:20
  85.7 1.0 broadcast_multiply_fusion
  86.7 2.7 fusion.4
  89.5 43.7 %reduce-scatter.2.cloned.1.call-done = f32[256,1024]{1,0:T(8,128)} async-done(((f32[256,4096]{1,0:T(8,128)}), f32[256,1024]{1,0:T(8,128)}) %reduce-scatter.2.cloned.1.call-update) | async-done | bytes 1048592 | tf_op jit(solution)/shard_map/reduce_scatter | solution.py:25
  133.2 1.5 multiply_subtract_fusion
  134.8 1.7 convolution_multiply_fusion
  136.5 129.4 %all-reduce.6.cloned.1.call-done = f32[256,256]{0,1:T(8,128)} async-done(((f32[256,256]{0,1:T(8,128)}), f32[256,256]{0,1:T(8,128)}) %all-reduce.6.cloned.1.call-update) | async-done | bytes 262160 | tf_op jit(solution)/shard_map/psum | solution.py:28
  265.9 1.1 copy.6
  267.0 1.0 fusion.2
  268.0 0.7 copy-done.3
  268.7 11.7 %cholesky.50 = f32[128,128]{1,0:T(8,128)S(1)} custom-call(f32[128,128]{1,0:T(8,128)S(1)} %cholesky.118), custom_call_target="Cholesky" | custom-call | tf_op jit(solution)/shard_map/jit(cholesky)/cholesky | solution.py:29
  280.5 9.8 %custom-call.14 = f32[1,128,128]{1,2,0:T(8,128)S(1)} custom-call(f32[1,128,128]{2,1,0:T(8,128)S(1)} %get-tuple-element.26), custom_call_target="InvertDiagBlocksLowerTriangular" | custom-call | tf_op jit(solution)/shard_map/jit(cholesky)/cholesky | solution.py:29
  290.3 1.0 constant_dynamic-update-slice_fusion.1
  291.4 1.1 convolution_subtract_fusion.1
  292.5 11.7 %cholesky.105 = f32[128,128]{1,0:T(8,128)S(1)} custom-call(f32[128,128]{1,0:T(8,128)S(1)} %convolution_subtract_fusion.1), custom_call_target="Cholesky" | custom-call | tf_op jit(solution)/shard_map/jit(cholesky)/cholesky | solution.py:29
  304.2 0.7 compare_reduce_fusion
  306.1 1.7 fusion.3
  307.9 5.0 %while.1 = (s32[]{:T(128)}, f32[256,256]{1,0:T(8,128)S(1)}, s32[2,2]{1,0:T(2,128)S(1)}, f32[2,128,128]{2,1,0:T(8,128)}, s32[]{:T(128)}) while((s32[]{:T(128)}, f32[256,256]{1,0:T(8,128)S(1)}, s32[2,2]{1,0:T(2,128)S(1)}, f32[2,128,128]{2,1,0:T(8,128)}, s32[]{:T(128)}) %tuple.29), condition=%wide.while_cond, body=%wide.while_body.sunk | while | flops 2 | bytes 132205 | solution.py:30
  308.5 1.9 bitcast_dynamic-update-slice_fusion.2
  311.0 1.9 bitcast_dynamic-update-slice_fusion.2
  312.9 20.5 %custom-call.15 = f32[2,128,128]{1,2,0:T(8,128)S(1)} custom-call(f32[2,128,128]{2,1,0:T(8,128)} %get-tuple-element.10), custom_call_target="InvertDiagBlocksLowerTriangular" | custom-call | tf_op jit(solution)/shard_map/triangular_solve | solution.py:30
  335.2 0.8 pad_maximum_fusion
  (26 shorter events, 3.4 us)
Async XLA Ops:
  7.2 1.6 copy-start
  7.2 78.5 %all-reduce.4.cloned.1.call-start = ((), (), s32[]{:S(2)}) async-start(), calls=%async_computation.1 | async-start | bytes 524288 | tf_op jit(solution)/shard_map/psum | solution.py:20
  11.8 121.4 %reduce-scatter.2.cloned.1.call-start = ((), (), s32[]{:S(2)}) async-start(), calls=%async_computation.2 | async-start | bytes 5242880 | tf_op jit(solution)/shard_map/reduce_scatter | solution.py:25
  86.7 2.7 copy-start.1
  89.4 176.5 %all-reduce.6.cloned.1.call-start = ((), (), s32[]{:S(2)}) async-start(), calls=%async_computation.3 | async-start | bytes 524288 | tf_op jit(solution)/shard_map/psum | solution.py:28
  268.0 0.7 copy-start.3
  304.2 1.9 copy-start.2
Sparse Core Ops, SparseCore 0:
  12.0 73.7 all-reduce.3
  89.5 43.6 reduce-scatter.1
  139.3 126.5 all-reduce.5
where the time goes:
time: 343 us
  waiting for transfers between devices  247 us (72%)
  other arithmetic  60.5 us (18%)
  between operations  15.1 us (4%)
  matrix products  11.5 us (3%)
  local copies, waits for them, and re-layouts  8.42 us (2%)
    psum x1, waiting for transfers between devices, shards(): gram = lax.psum(partial_gram, ('rows', 'cols'))  129 us
    psum x1, waiting for transfers between devices, shards(): coefficients = lax.psum(partial_value, 'rows') * coeff_scale  73.8 us
    reduce_scatter x1, waiting for transfers between devices, shards(): lax.psum_scatter(recon_part, 'cols', scatter_dimension=1, tiled=True)  43.7 us
    another operation x6, other arithmetic, shards(): factor = jnp.linalg.cholesky(gram)  34 us
    another operation x4, other arithmetic, shards(): lax.linalg.triangular_solve(factor, residual, left_side=True, lower=True)  23 us
  transfers between devices with their start and end apart: 3, of which 3 were waited for; matrix products, arithmetic and copies ran while one was open for 0% of the time, Pallas kernels for 0%

commit v1 on v0

--- a/solution.py
+++ b/solution.py
@@ -5,6 +5,11 @@
 from jax.sharding import PartitionSpec as P
 
 RANK = 1024
+
+
+def axis_by_axis(array, first, second):
+    inner = lax.psum(array, first)
+    return lax.psum(inner, second)
 
 
 def shards(basis_cols, snapshots):
@@ -25,7 +30,7 @@
     recon = lax.psum_scatter(recon_part, "cols", scatter_dimension=1, tiled=True) / math.sqrt(RANK)
     residual = own_snaps.astype(jnp.float32) - recon
     partial_gram = jnp.dot(residual, residual.T, precision=lax.Precision.HIGHEST) / total_points
-    gram = lax.psum(partial_gram, ("rows", "cols"))
+    gram = axis_by_axis(partial_gram, "rows", "cols")
     factor = jnp.linalg.cholesky(gram)
     directions = lax.linalg.triangular_solve(factor, residual, left_side=True, lower=True).astype(
         jnp.bfloat16

time: 343 us -> 319 us (0.930)
  waiting for transfers between devices: 247 us -> 223 us
    psum x1 -> x2, waiting for transfers between devices: 129 us -> 105 us  [the longest x1 71.5 us: axis_by_axis(): inner = lax.psum(array, first)]
  transfers between devices with their start and end apart: 3 -> 4, of which waited for: 3 -> 4; matrix products, arithmetic and copies ran while one was open for 0% -> 0% of each run, Pallas kernels for 0% -> 0%
where the time goes in v1:
time: 319 us
  waiting for transfers between devices  223 us (70%)
  other arithmetic  60.5 us (19%)
  between operations  15.1 us (5%)
  matrix products  11.5 us (4%)
  local copies, waits for them, and re-layouts  8.42 us (3%)
    psum x1, waiting for transfers between devices, shards(): coefficients = lax.psum(partial_value, 'rows') * coeff_scale  73.8 us
    psum x1, waiting for transfers between devices, axis_by_axis(): inner = lax.psum(array, first)  71.5 us
    reduce_scatter x1, waiting for transfers between devices, shards(): lax.psum_scatter(recon_part, 'cols', scatter_dimension=1, tiled=True)  43.7 us
    another operation x6, other arithmetic, shards(): factor = jnp.linalg.cholesky(gram)  34 us
    psum x1, waiting for transfers between devices, axis_by_axis(): return lax.psum(inner, second)  33.7 us
    another operation x4, other arithmetic, shards(): lax.linalg.triangular_solve(factor, residual, left_side=True, lower=True)  23 us
  transfers between devices with their start and end apart: 4, of which 4 were waited for; matrix products, arithmetic and copies ran while one was open for 0% of the time, Pallas kernels for 0%

profile of v1, /device:TPU:0, one launch (start us, length us, event | category | flops | bytes accessed | tf_op | source)
XLA Modules:
  0.0 318.6 jit_solution(7522622275943679476)
XLA Ops:
  7.2 1.5 copy-done
  8.8 3.0 fusion.12
  11.9 73.8 %all-reduce.5.cloned.1.call-done = f32[256,256]{1,0:T(8,128)} async-done(((f32[256,256]{1,0:T(8,128)}), f32[256,256]{1,0:T(8,128)}) %all-reduce.5.cloned.1.call-update) | async-done | bytes 262160 | tf_op jit(solution)/shard_map/psum | solution.py:25
  85.7 1.0 broadcast_multiply_fusion
  86.7 2.7 fusion.4
  89.5 43.7 %reduce-scatter.2.cloned.1.call-done = f32[256,1024]{1,0:T(8,128)} async-done(((f32[256,4096]{1,0:T(8,128)}), f32[256,1024]{1,0:T(8,128)}) %reduce-scatter.2.cloned.1.call-update) | async-done | bytes 1048592 | tf_op jit(solution)/shard_map/reduce_scatter | solution.py:30
  133.2 1.5 multiply_subtract_fusion
  134.8 1.7 convolution_multiply_fusion
  136.8 71.5 %all-reduce.7.cloned.1.call-done = f32[256,256]{0,1:T(8,128)} async-done(((f32[256,256]{0,1:T(8,128)}), f32[256,256]{0,1:T(8,128)}) %all-reduce.7.cloned.1.call-update) | async-done | bytes 262160 | tf_op jit(solution)/shard_map/psum | solution.py:11
  208.3 33.7 %all-reduce.9.cloned.1.call-done = f32[256,256]{0,1:T(8,128)} async-done(((f32[256,256]{0,1:T(8,128)}), f32[256,256]{0,1:T(8,128)}) %all-reduce.9.cloned.1.call-update) | async-done | bytes 262160 | tf_op jit(solution)/shard_map/psum | solution.py:12
  241.9 1.1 copy.6
  243.0 1.0 fusion.2
  244.0 0.7 copy-done.3
  244.7 11.7 %cholesky.50 = f32[128,128]{1,0:T(8,128)S(1)} custom-call(f32[128,128]{1,0:T(8,128)S(1)} %cholesky.118), custom_call_target="Cholesky" | custom-call | tf_op jit(solution)/shard_map/jit(cholesky)/cholesky | solution.py:34
  256.5 9.8 %custom-call.14 = f32[1,128,128]{1,2,0:T(8,128)S(1)} custom-call(f32[1,128,128]{2,1,0:T(8,128)S(1)} %get-tuple-element.26), custom_call_target="InvertDiagBlocksLowerTriangular" | custom-call | tf_op jit(solution)/shard_map/jit(cholesky)/cholesky | solution.py:34
  266.3 1.0 constant_dynamic-update-slice_fusion.1
  267.4 1.1 convolution_subtract_fusion.1
  268.5 11.7 %cholesky.105 = f32[128,128]{1,0:T(8,128)S(1)} custom-call(f32[128,128]{1,0:T(8,128)S(1)} %convolution_subtract_fusion.1), custom_call_target="Cholesky" | custom-call | tf_op jit(solution)/shard_map/jit(cholesky)/cholesky | solution.py:34
  282.1 1.7 fusion.3
  283.9 5.0 %while.1 = (s32[]{:T(128)}, f32[256,256]{1,0:T(8,128)S(1)}, s32[2,2]{1,0:T(2,128)S(1)}, f32[2,128,128]{2,1,0:T(8,128)}, s32[]{:T(128)}) while((s32[]{:T(128)}, f32[256,256]{1,0:T(8,128)S(1)}, s32[2,2]{1,0:T(2,128)S(1)}, f32[2,128,128]{2,1,0:T(8,128)}, s32[]{:T(128)}) %tuple.29), condition=%wide.while_cond, body=%wide.while_body.sunk | while | flops 2 | bytes 132205 | solution.py:35
  284.5 1.9 bitcast_dynamic-update-slice_fusion.2
  287.0 1.9 bitcast_dynamic-update-slice_fusion.2
  288.9 20.5 %custom-call.15 = f32[2,128,128]{1,2,0:T(8,128)S(1)} custom-call(f32[2,128,128]{2,1,0:T(8,128)} %get-tuple-element.10), custom_call_target="InvertDiagBlocksLowerTriangular" | custom-call | tf_op jit(solution)/shard_map/triangular_solve | solution.py:35
  311.3 0.8 pad_maximum_fusion
  (29 shorter events, 4.3 us)
Async XLA Ops:
  7.2 1.6 copy-start
  7.2 78.5 %all-reduce.5.cloned.1.call-start = ((), (), s32[]{:S(2)}) async-start(), calls=%async_computation.1 | async-start | bytes 524288 | tf_op jit(solution)/shard_map/psum | solution.py:25
  11.8 121.4 %reduce-scatter.2.cloned.1.call-start = ((), (), s32[]{:S(2)}) async-start(), calls=%async_computation.2 | async-start | bytes 5242880 | tf_op jit(solution)/shard_map/reduce_scatter | solution.py:30
  86.7 2.7 copy-start.1
  89.4 118.8 %all-reduce.7.cloned.1.call-start = ((), (), s32[]{:S(2)}) async-start(), calls=%async_computation.3 | async-start | bytes 524288 | tf_op jit(solution)/shard_map/psum | solution.py:11
  136.5 105.4 %all-reduce.9.cloned.1.call-start = ((), (), s32[]{:S(2)}) async-start(), calls=%async_computation.4 | async-start | bytes 524288 | tf_op jit(solution)/shard_map/psum | solution.py:12
  244.0 0.7 copy-start.3
  280.2 1.9 copy-start.2
Sparse Core Ops, SparseCore 0:
  12.0 73.7 all-reduce.4
  89.5 43.6 reduce-scatter.1
  137.2 71.0 all-reduce.6
  210.4 31.4 all-reduce.8
